TPU v7x, 1024 devices: a whole 4x4x32 slice. The times are simulated.
1024 devices in a mesh: sec: 4 (over x), gx: 64 (over z_lo, y), gz: 4 (over z_hi, core).
Axes of the slice: x: 4, y: 4, z: 32 (z_hi: 2, z_lo: 16; z = z_hi * 16 + z_lo), core: 2. Of those that a mesh axis runs over, the one named last changes fastest.
Arguments:
- fields: float32 [4, 5, 8192, 512], P('sec', None, 'gx', 'gz'), may hold values from -6 to 6
- media: float32 [4, 3, 8192, 512], P('sec', None, 'gx', 'gz'), may hold values from 0.5 to 2
- plane_rows: int32 [32], replicated, may hold values from 0 to 511, as said below
- box_offset: int32 [3], replicated, may hold values from 0 to 256
Outputs:
- evolved: float32 [4, 5, 8192, 512], P('sec', None, 'gx', 'gz')
Inputs may be any that keep to these rules, and one draw needn't show every extreme that they name: `plane_rows`: entries 8 * j to 8 * j + 7 are distinct rows of the j-th depth block of 128 rows; row 0 and row 511 are always among them.
All inputs are finite; a program needn't handle non-finite values.
Results may differ from a plain program's by a relative error of at most 0.00013.
Values sent between devices are 32-bit elements; how exact they have to be, the bound alone decides.
A program may use at most 32 MiB of HBM per device.

v0:
```python
import jax
import jax.numpy as jnp
from jax import lax
from jax.sharding import PartitionSpec as P

RADIUS = 4
STEPS = 5
NPD = 8


STENCIL = (0.8, -0.2, 4.0 / 105.0, -1.0 / 280.0)
TIME_STEP = 0.2
COUPLING = 0.5
RELAXATION = (0.9, 0.5)
MEMORY_WEIGHT = (0.15, 0.1)


def padded_2(block, sides, width):
    for axis, dim in sides:
        count = lax.axis_size(axis)
        forward = [(i, i + 1) for i in range(count - 1)]
        backward = [(target, source) for source, target in forward]
        low = lax.ppermute(
            lax.slice_in_dim(block, block.shape[dim] - width, None, axis=dim), axis, forward
        )
        high = lax.ppermute(lax.slice_in_dim(block, 0, width, axis=dim), axis, backward)
        block = jnp.concatenate([low, block, high], axis=dim)
    return block


def broadcast(value, axis, source):
    kept = jnp.where(lax.axis_index(axis) == source, value, 0).astype(value.dtype)
    return lax.psum(kept, axis)


def along_x(padded, anchor, count_x, count_z):
    summed = jnp.zeros(padded.shape[:-2] + (count_x, count_z), jnp.float32)
    for offset, stencil_tap in enumerate(STENCIL, 1):
        forward = padded[
            ..., anchor + offset : anchor + offset + count_x, anchor : anchor + count_z
        ]
        backward = padded[
            ..., anchor - offset : anchor - offset + count_x, anchor : anchor + count_z
        ]
        summed = summed + stencil_tap * (forward - backward)
    return summed


def along_z(padded, anchor, count_x, count_z):
    summed = jnp.zeros(padded.shape[:-2] + (count_x, count_z), jnp.float32)
    for offset, stencil_tap in enumerate(STENCIL, 1):
        forward = padded[
            ..., anchor : anchor + count_x, anchor + offset : anchor + offset + count_z
        ]
        backward = padded[
            ..., anchor : anchor + count_x, anchor - offset : anchor - offset + count_z
        ]
        summed = summed + stencil_tap * (forward - backward)
    return summed


def velocity_elastic(velocity, stresses, buoyancy, anchor, count_x, count_z):
    updated_x = velocity[0] + TIME_STEP * buoyancy * (
        along_x(stresses[0], anchor, count_x, count_z)
        + along_z(stresses[2], anchor, count_x, count_z)
    )
    updated_z = velocity[1] + TIME_STEP * buoyancy * (
        along_x(stresses[2], anchor, count_x, count_z)
        + along_z(stresses[1], anchor, count_x, count_z)
    )
    return jnp.stack([updated_x, updated_z])


def velocity_acoustic(velocity, stresses, buoyancy, anchor, count_x, count_z):
    updated_x = velocity[0] - TIME_STEP * buoyancy * along_x(stresses[0], anchor, count_x, count_z)
    updated_z = velocity[1] - TIME_STEP * buoyancy * along_z(stresses[0], anchor, count_x, count_z)
    return jnp.stack([updated_x, updated_z])


def stress_elastic(stresses, velocity_pad, material, anchor, count_x, count_z):
    strain_x = along_x(velocity_pad[0], anchor, count_x, count_z)
    strain_z = along_z(velocity_pad[1], anchor, count_x, count_z)
    strain_shear = along_z(velocity_pad[0], anchor, count_x, count_z) + along_x(
        velocity_pad[1], anchor, count_x, count_z
    )
    lame_first = material[1]
    shear_modulus = material[2]
    normal_x = stresses[0] + TIME_STEP * (
        (lame_first + 2.0 * shear_modulus) * strain_x + lame_first * strain_z
    )
    normal_z = stresses[1] + TIME_STEP * (
        lame_first * strain_x + (lame_first + 2.0 * shear_modulus) * strain_z
    )
    shear_new = stresses[2] + TIME_STEP * shear_modulus * strain_shear
    return jnp.stack([normal_x, normal_z, shear_new])


def stress_acoustic(stresses, velocity_pad, material, anchor, count_x, count_z):
    divergence = along_x(velocity_pad[0], anchor, count_x, count_z) + along_z(
        velocity_pad[1], anchor, count_x, count_z
    )
    loading = material[1] * divergence
    memory_one = (
        RELAXATION[0] * stresses[1]
        + (1.0 - RELAXATION[0]) * MEMORY_WEIGHT[0] * material[2] * loading
    )
    memory_two = (
        RELAXATION[1] * stresses[2]
        + (1.0 - RELAXATION[1]) * MEMORY_WEIGHT[1] * material[2] * loading
    )
    pressure = stresses[0] - TIME_STEP * (loading - memory_one - memory_two)
    return jnp.stack([pressure, memory_one, memory_two])


def local(fields, media, plane_rows, box_offset):
    current = fields[0]
    material = media[0]
    count_x = current.shape[1]
    count_z = current.shape[2]
    section = lax.axis_index("sec")
    is_source = section == 0
    block_z = lax.axis_index("gz")
    local_rows = lax.dynamic_slice_in_dim(plane_rows, block_z * NPD, NPD) - block_z * count_z
    offset = lax.dynamic_slice_in_dim(box_offset, jnp.maximum(section - 1, 0), 1)[0]
    depth_ids = block_z * count_z + jnp.arange(count_z, dtype=jnp.int32)
    landing = offset + plane_rows // 2
    chosen = (landing[:, None] == depth_ids[None, :]).astype(jnp.float32)
    for step_index in range(STEPS):
        stress_pad = padded_2(current[2:5], (("gx", 1), ("gz", 2)), RADIUS)
        velocity = lax.cond(
            is_source,
            lambda: velocity_elastic(
                current[0:2], stress_pad, material[0], RADIUS, count_x, count_z
            ),
            lambda: velocity_acoustic(
                current[0:2], stress_pad, material[0], RADIUS, count_x, count_z
            ),
        )
        velocity_pad = padded_2(velocity, (("gx", 1), ("gz", 2)), RADIUS)
        stresses = lax.cond(
            is_source,
            lambda: stress_elastic(current[2:5], velocity_pad, material, RADIUS, count_x, count_z),
            lambda: stress_acoustic(current[2:5], velocity_pad, material, RADIUS, count_x, count_z),
        )
        current = jnp.concatenate([velocity, stresses], axis=0)
        picked = jnp.take(current, local_rows, axis=2)
        block_plane = jnp.transpose(
            jnp.stack([picked[0], picked[1], -0.5 * (picked[2] + picked[3])]), (0, 2, 1)
        )
        joined = lax.all_gather(block_plane, "gz", axis=1, tiled=True)
        gathered = broadcast(joined, "sec", 0)
        injected = jnp.einsum("ckx,kz->cxz", gathered, chosen, precision=lax.Precision.HIGHEST)
        far_state = jnp.concatenate([current[0:3] + COUPLING * injected, current[3:5]], axis=0)
        current = jnp.where(is_source, current, far_state)
    return current[None]


def solution(mesh):
    in_specs = (P("sec", None, "gx", "gz"), P("sec", None, "gx", "gz"), P(), P())
    out_specs = P("sec", None, "gx", "gz")
    return jax.shard_map(local, mesh=mesh, in_specs=in_specs, out_specs=out_specs, check_vma=False)
```

profile of v0, /device:TPU:32, one launch (start us, length us, event | category | flops | bytes accessed | tf_op | source)
XLA Modules:
  0.0 681.9 jit_solution(13985893738908478812)
XLA Ops:
  1.0 3.5 collective-permute-start
  4.4 4.5 collective-permute-start.1
  11.7 1.3 collective-permute-start.2
  13.0 1.3 collective-permute-start.3
  14.4 28.3 %collective-permute-done.3 = f32[3,136,4]{2,1,0:T(8,128)S(1)} collective-permute-done((f32[3,136,4]{2,1,0:T(8,128)S(1)}, f32[3,136,4]{2,1,0:T(8,128)S(1)}, u32[]{:S(2)}, u32[]{:S(2)}) %collective-permute-start.3) | collective-permute-done | bytes 6560 | tf_op jit(solution)/shard_map/ppermute | solution.py:26
  43.7 1.9 collective-permute-start.4
  45.7 6.0 collective-permute-start.5
  53.1 37.1 %collective-permute-start.6 = (f32[2,136,4]{2,1,0:T(8,128)S(1)}, f32[2,136,4]{2,1,0:T(8,128)S(1)}, u32[]{:S(2)}, u32[]{:S(2)}) collective-permute-start(f32[2,136,4]{2,1,0:T(8,128)S(1)} %get-tuple-element.316), channel_id=1, source_target_pairs={{0,1},{1,2},{2,3},{4,5},{5,6},{6,7},{8,9},{9,10},{10,11},{12,13},{... | collective-permute-start | bytes 13064 | tf_op jit(solution)/shard_map/ppermute | solution.py:23
  90.2 1.3 collective-permute-start.7
  91.5 3.4 collective-permute-done.7
  96.8 48.3 %all_gather.15 = f32[3,32,128]{2,1,0:T(8,128)S(1)} all-gather(f32[3,8,128]{2,1,0:T(8,128)S(1)} %maximum_bitcast_fusion), channel_id=1, replica_groups=mesh['sec'=4,'gx'=64,'gz'=4] {'gz'}, dimensions={1}, use_global_device_ids=true | all-gather | bytes 61440 | tf_op jit(solution)/shard_map/all_gather | solution.py:150
  145.1 16.8 %psum.35 = f32[3,32,128]{2,1,0:T(8,128)S(1)} all-reduce(f32[3,32,128]{2,1,0:T(8,128)S(1)} %broadcast_select_fusion.4), channel_id=1, replica_groups=mesh['sec'=4,'gx'=64,'gz'=4] {'sec'}, use_global_device_ids=true, to_apply=%region_4.6 | all-reduce | flops 12288 | bytes 98304 | tf_op jit(solution)/shard_map/psum | solution.py:33
  162.3 6.2 collective-permute-start.8
  168.6 1.9 collective-permute-start.9
  170.5 3.6 collective-permute-done.9
  174.2 1.3 collective-permute-start.10
  175.5 1.3 collective-permute-start.11
  176.8 3.5 collective-permute-done.11
  181.3 1.9 collective-permute-start.12
  183.3 6.0 collective-permute-start.13
  189.3 1.3 collective-permute-done.13
  190.7 34.6 %collective-permute-start.14 = (f32[2,136,4]{2,1,0:T(8,128)S(1)}, f32[2,136,4]{2,1,0:T(8,128)S(1)}, u32[]{:S(2)}, u32[]{:S(2)}) collective-permute-start(f32[2,136,4]{2,1,0:T(8,128)S(1)} %get-tuple-element.314), channel_id=1, source_target_pairs={{0,1},{1,2},{2,3},{4,5},{5,6},{6,7},{8,9},{9,10},{10,11},{12,13},{... | collective-permute-start | bytes 13064 | tf_op jit(solution)/shard_map/ppermute | solution.py:23
  225.3 1.3 collective-permute-start.15
  226.6 3.4 collective-permute-done.15
  231.9 49.1 %all_gather.16 = f32[3,32,128]{2,1,0:T(8,128)S(1)} all-gather(f32[3,8,128]{2,1,0:T(8,128)S(1)} %maximum_bitcast_fusion.1), channel_id=1, replica_groups=mesh['sec'=4,'gx'=64,'gz'=4] {'gz'}, dimensions={1}, use_global_device_ids=true | all-gather | bytes 61440 | tf_op jit(solution)/shard_map/all_gather | solution.py:150
  281.0 14.7 %psum.36 = f32[3,32,128]{2,1,0:T(8,128)S(1)} all-reduce(f32[3,32,128]{2,1,0:T(8,128)S(1)} %broadcast_select_fusion.3), channel_id=1, replica_groups=mesh['sec'=4,'gx'=64,'gz'=4] {'sec'}, use_global_device_ids=true, to_apply=%region_9.11 | all-reduce | flops 12288 | bytes 98304 | tf_op jit(solution)/shard_map/psum | solution.py:33
  296.1 1.9 collective-permute-start.16
  298.0 6.0 collective-permute-start.17
  304.1 1.3 collective-permute-done.17
  305.5 1.3 collective-permute-start.18
  306.9 1.3 collective-permute-start.19
  308.2 4.5 collective-permute-done.19
  313.7 2.5 collective-permute-start.20
  316.2 5.8 collective-permute-start.21
  323.4 30.6 %collective-permute-start.22 = (f32[2,136,4]{2,1,0:T(8,128)S(1)}, f32[2,136,4]{2,1,0:T(8,128)S(1)}, u32[]{:S(2)}, u32[]{:S(2)}) collective-permute-start(f32[2,136,4]{2,1,0:T(8,128)S(1)} %get-tuple-element.312), channel_id=1, source_target_pairs={{0,1},{1,2},{2,3},{4,5},{5,6},{6,7},{8,9},{9,10},{10,11},{12,13},{... | collective-permute-start | bytes 13064 | tf_op jit(solution)/shard_map/ppermute | solution.py:23
  353.9 1.3 collective-permute-start.23
  355.3 4.3 collective-permute-done.23
  361.6 46.9 %all_gather.17 = f32[3,32,128]{2,1,0:T(8,128)S(1)} all-gather(f32[3,8,128]{2,1,0:T(8,128)S(1)} %maximum_bitcast_fusion.2), channel_id=1, replica_groups=mesh['sec'=4,'gx'=64,'gz'=4] {'gz'}, dimensions={1}, use_global_device_ids=true | all-gather | bytes 61440 | tf_op jit(solution)/shard_map/all_gather | solution.py:150
  408.5 16.0 %psum.37 = f32[3,32,128]{2,1,0:T(8,128)S(1)} all-reduce(f32[3,32,128]{2,1,0:T(8,128)S(1)} %broadcast_select_fusion.2), channel_id=1, replica_groups=mesh['sec'=4,'gx'=64,'gz'=4] {'sec'}, use_global_device_ids=true, to_apply=%region_14.16 | all-reduce | flops 12288 | bytes 98304 | tf_op jit(solution)/shard_map/psum | solution.py:33
  425.0 5.1 collective-permute-start.24
  430.1 2.9 collective-permute-start.25
  433.0 2.6 collective-permute-done.25
  435.7 1.3 collective-permute-start.26
  438.4 3.6 collective-permute-done.27
  442.9 1.9 collective-permute-start.28
  444.9 6.0 collective-permute-start.29
  450.9 1.3 collective-permute-done.29
  452.3 28.9 %collective-permute-start.30 = (f32[2,136,4]{2,1,0:T(8,128)S(1)}, f32[2,136,4]{2,1,0:T(8,128)S(1)}, u32[]{:S(2)}, u32[]{:S(2)}) collective-permute-start(f32[2,136,4]{2,1,0:T(8,128)S(1)} %get-tuple-element.310), channel_id=1, source_target_pairs={{0,1},{1,2},{2,3},{4,5},{5,6},{6,7},{8,9},{9,10},{10,11},{12,13},{... | collective-permute-start | bytes 13064 | tf_op jit(solution)/shard_map/ppermute | solution.py:23
  482.5 4.3 collective-permute-done.31
  488.8 45.8 %all_gather.18 = f32[3,32,128]{2,1,0:T(8,128)S(1)} all-gather(f32[3,8,128]{2,1,0:T(8,128)S(1)} %maximum_bitcast_fusion.3), channel_id=1, replica_groups=mesh['sec'=4,'gx'=64,'gz'=4] {'gz'}, dimensions={1}, use_global_device_ids=true | all-gather | bytes 61440 | tf_op jit(solution)/shard_map/all_gather | solution.py:150
  534.6 14.7 %psum.38 = f32[3,32,128]{2,1,0:T(8,128)S(1)} all-reduce(f32[3,32,128]{2,1,0:T(8,128)S(1)} %broadcast_select_fusion.1), channel_id=1, replica_groups=mesh['sec'=4,'gx'=64,'gz'=4] {'sec'}, use_global_device_ids=true, to_apply=%region_19.21 | all-reduce | flops 12288 | bytes 98304 | tf_op jit(solution)/shard_map/psum | solution.py:33
  549.7 6.8 collective-permute-start.32
  556.5 1.9 collective-permute-start.33
  558.4 3.6 collective-permute-done.33
  562.2 1.3 collective-permute-start.34
  563.5 1.3 collective-permute-start.35
  564.8 3.6 collective-permute-done.35
  569.3 1.9 collective-permute-start.36
  571.3 6.0 collective-permute-start.37
  577.3 1.3 collective-permute-done.37
  578.7 29.1 %collective-permute-start.38 = (f32[2,136,4]{2,1,0:T(8,128)S(1)}, f32[2,136,4]{2,1,0:T(8,128)S(1)}, u32[]{:S(2)}, u32[]{:S(2)}) collective-permute-start(f32[2,136,4]{2,1,0:T(8,128)S(1)} %get-tuple-element.308), channel_id=1, source_target_pairs={{0,1},{1,2},{2,3},{4,5},{5,6},{6,7},{8,9},{9,10},{10,11},{12,13},{... | collective-permute-start | bytes 13064 | tf_op jit(solution)/shard_map/ppermute | solution.py:23
  609.1 3.5 collective-permute-done.39
  614.5 44.5 %all_gather.19 = f32[3,32,128]{2,1,0:T(8,128)S(1)} all-gather(f32[3,8,128]{2,1,0:T(8,128)S(1)} %maximum_bitcast_fusion.4), channel_id=1, replica_groups=mesh['sec'=4,'gx'=64,'gz'=4] {'gz'}, dimensions={1}, use_global_device_ids=true | all-gather | bytes 61440 | tf_op jit(solution)/shard_map/all_gather | solution.py:150
  659.1 21.7 %psum.39 = f32[3,32,128]{2,1,0:T(8,128)S(1)} all-reduce(f32[3,32,128]{2,1,0:T(8,128)S(1)} %broadcast_select_fusion), channel_id=1, replica_groups=mesh['sec'=4,'gx'=64,'gz'=4] {'sec'}, use_global_device_ids=true, to_apply=%region_24.26 | all-reduce | flops 12288 | bytes 98304 | tf_op jit(solution)/shard_map/psum | solution.py:33
  (194 shorter events, 35.7 us)
Async XLA Ops:
  1.0 10.5 %collective-permute-start = (f32[3,4,128]{2,1,0:T(4,128)S(1)}, f32[3,4,128]{2,1,0:T(4,128)S(1)}, u32[]{:S(2)}, u32[]{:S(2)}) collective-permute-start(f32[3,4,128]{2,1,0:T(4,128)S(1)} %get-tuple-element.306), channel_id=1, source_target_pairs={{0,4},{4,8},{8,12},{12,16},{16,20},{20,24},{24,28},{28,32},{32,36}... | collective-permute-start | bytes 18440 | tf_op jit(solution)/shard_map/ppermute | solution.py:23
  4.4 7.1 %collective-permute-start.1 = (f32[3,4,128]{2,1,0:T(4,128)S(1)}, f32[3,4,128]{2,1,0:T(4,128)S(1)}, u32[]{:S(2)}, u32[]{:S(2)}) collective-permute-start(f32[3,4,128]{2,1,0:T(4,128)S(1)} %get-tuple-element.307), channel_id=1, source_target_pairs={{4,0},{8,4},{12,8},{16,12},{20,16},{24,20},{28,24},{32,28},{36,32}... | collective-permute-start | bytes 18440 | tf_op jit(solution)/shard_map/ppermute | solution.py:26
  8.9 0.7 copy-start.3
  10.2 0.7 copy-start.2
  11.7 2.7 collective-permute-start.2
  13.0 29.7 %collective-permute-start.3 = (f32[3,136,4]{2,1,0:T(8,128)S(1)}, f32[3,136,4]{2,1,0:T(8,128)S(1)}, u32[]{:S(2)}, u32[]{:S(2)}) collective-permute-start(f32[3,136,4]{2,1,0:T(8,128)S(1)} %get-tuple-element.305), channel_id=1, source_target_pairs={{1,0},{2,1},{3,2},{5,4},{6,5},{7,6},{9,8},{10,9},{11,10},{13,12},{... | collective-permute-start | bytes 19592 | tf_op jit(solution)/shard_map/ppermute | solution.py:26
  14.4 28.6 %copy-start = (f32[1,3,128,128]{3,2,1,0:T(8,128)S(1)}, f32[1,3,128,128]{3,2,1,0:T(8,128)}, u32[]{:S(2)}) copy-start(f32[1,3,128,128]{3,2,1,0:T(8,128)} %param.27) | copy-start | bytes 589828
  14.4 28.6 %copy-start.1 = (f32[1,5,128,128]{3,2,1,0:T(8,128)S(1)}, f32[1,5,128,128]{3,2,1,0:T(8,128)}, u32[]{:S(2)}) copy-start(f32[1,5,128,128]{3,2,1,0:T(8,128)} %param.26) | copy-start | bytes 983044
  43.7 8.0 %collective-permute-start.4 = (f32[2,4,128]{2,1,0:T(4,128)S(1)}, f32[2,4,128]{2,1,0:T(4,128)S(1)}, u32[]{:S(2)}, u32[]{:S(2)}) collective-permute-start(f32[2,4,128]{2,1,0:T(4,128)S(1)} %get-tuple-element.326), channel_id=1, source_target_pairs={{0,4},{4,8},{8,12},{12,16},{16,20},{20,24},{24,28},{28,32},{32,36}... | collective-permute-start | bytes 12296 | tf_op jit(solution)/shard_map/ppermute | solution.py:23
  45.7 7.3 %collective-permute-start.5 = (f32[2,4,128]{2,1,0:T(4,128)S(1)}, f32[2,4,128]{2,1,0:T(4,128)S(1)}, u32[]{:S(2)}, u32[]{:S(2)}) collective-permute-start(f32[2,4,128]{2,1,0:T(4,128)S(1)} %get-tuple-element.327), channel_id=1, source_target_pairs={{4,0},{8,4},{12,8},{16,12},{20,16},{24,20},{28,24},{32,28},{36,32}... | collective-permute-start | bytes 12296 | tf_op jit(solution)/shard_map/ppermute | solution.py:26
  53.1 38.4 %collective-permute-start.6 = (f32[2,136,4]{2,1,0:T(8,128)S(1)}, f32[2,136,4]{2,1,0:T(8,128)S(1)}, u32[]{:S(2)}, u32[]{:S(2)}) collective-permute-start(f32[2,136,4]{2,1,0:T(8,128)S(1)} %get-tuple-element.316), channel_id=1, source_target_pairs={{0,1},{1,2},{2,3},{4,5},{5,6},{6,7},{8,9},{9,10},{10,11},{12,13},{... | collective-permute-start | bytes 13064 | tf_op jit(solution)/shard_map/ppermute | solution.py:23
  90.2 4.7 collective-permute-start.7
  162.3 8.2 %collective-permute-start.8 = (f32[3,4,128]{2,1,0:T(4,128)S(1)}, f32[3,4,128]{2,1,0:T(4,128)S(1)}, u32[]{:S(2)}, u32[]{:S(2)}) collective-permute-start(f32[3,4,128]{2,1,0:T(4,128)S(1)} %get-tuple-element.294), channel_id=1, source_target_pairs={{0,4},{4,8},{8,12},{12,16},{16,20},{20,24},{24,28},{28,32},{32,36}... | collective-permute-start | bytes 18440 | tf_op jit(solution)/shard_map/ppermute | solution.py:23
  168.6 5.5 collective-permute-start.9
  174.2 2.6 collective-permute-start.10
  175.5 4.8 collective-permute-start.11
  181.3 8.0 %collective-permute-start.12 = (f32[2,4,128]{2,1,0:T(4,128)S(1)}, f32[2,4,128]{2,1,0:T(4,128)S(1)}, u32[]{:S(2)}, u32[]{:S(2)}) collective-permute-start(f32[2,4,128]{2,1,0:T(4,128)S(1)} %get-tuple-element.324), channel_id=1, source_target_pairs={{0,4},{4,8},{8,12},{12,16},{16,20},{20,24},{24,28},{28,32},{32,36}... | collective-permute-start | bytes 12296 | tf_op jit(solution)/shard_map/ppermute | solution.py:23
  183.3 7.3 %collective-permute-start.13 = (f32[2,4,128]{2,1,0:T(4,128)S(1)}, f32[2,4,128]{2,1,0:T(4,128)S(1)}, u32[]{:S(2)}, u32[]{:S(2)}) collective-permute-start(f32[2,4,128]{2,1,0:T(4,128)S(1)} %get-tuple-element.325), channel_id=1, source_target_pairs={{4,0},{8,4},{12,8},{16,12},{20,16},{24,20},{28,24},{32,28},{36,32}... | collective-permute-start | bytes 12296 | tf_op jit(solution)/shard_map/ppermute | solution.py:26
  190.7 35.9 %collective-permute-start.14 = (f32[2,136,4]{2,1,0:T(8,128)S(1)}, f32[2,136,4]{2,1,0:T(8,128)S(1)}, u32[]{:S(2)}, u32[]{:S(2)}) collective-permute-start(f32[2,136,4]{2,1,0:T(8,128)S(1)} %get-tuple-element.314), channel_id=1, source_target_pairs={{0,1},{1,2},{2,3},{4,5},{5,6},{6,7},{8,9},{9,10},{10,11},{12,13},{... | collective-permute-start | bytes 13064 | tf_op jit(solution)/shard_map/ppermute | solution.py:23
  225.3 4.7 collective-permute-start.15
  296.1 8.0 %collective-permute-start.16 = (f32[3,4,128]{2,1,0:T(4,128)S(1)}, f32[3,4,128]{2,1,0:T(4,128)S(1)}, u32[]{:S(2)}, u32[]{:S(2)}) collective-permute-start(f32[3,4,128]{2,1,0:T(4,128)S(1)} %get-tuple-element.292), channel_id=1, source_target_pairs={{0,4},{4,8},{8,12},{12,16},{16,20},{20,24},{24,28},{28,32},{32,36}... | collective-permute-start | bytes 18440 | tf_op jit(solution)/shard_map/ppermute | solution.py:23
  298.0 7.4 %collective-permute-start.17 = (f32[3,4,128]{2,1,0:T(4,128)S(1)}, f32[3,4,128]{2,1,0:T(4,128)S(1)}, u32[]{:S(2)}, u32[]{:S(2)}) collective-permute-start(f32[3,4,128]{2,1,0:T(4,128)S(1)} %get-tuple-element.293), channel_id=1, source_target_pairs={{4,0},{8,4},{12,8},{16,12},{20,16},{24,20},{28,24},{32,28},{36,32}... | collective-permute-start | bytes 18440 | tf_op jit(solution)/shard_map/ppermute | solution.py:26
  305.5 2.6 collective-permute-start.18
  306.9 5.8 collective-permute-start.19
  313.7 8.3 %collective-permute-start.20 = (f32[2,4,128]{2,1,0:T(4,128)S(1)}, f32[2,4,128]{2,1,0:T(4,128)S(1)}, u32[]{:S(2)}, u32[]{:S(2)}) collective-permute-start(f32[2,4,128]{2,1,0:T(4,128)S(1)} %get-tuple-element.322), channel_id=1, source_target_pairs={{0,4},{4,8},{8,12},{12,16},{16,20},{20,24},{24,28},{28,32},{32,36}... | collective-permute-start | bytes 12296 | tf_op jit(solution)/shard_map/ppermute | solution.py:23
  316.2 7.1 %collective-permute-start.21 = (f32[2,4,128]{2,1,0:T(4,128)S(1)}, f32[2,4,128]{2,1,0:T(4,128)S(1)}, u32[]{:S(2)}, u32[]{:S(2)}) collective-permute-start(f32[2,4,128]{2,1,0:T(4,128)S(1)} %get-tuple-element.323), channel_id=1, source_target_pairs={{4,0},{8,4},{12,8},{16,12},{20,16},{24,20},{28,24},{32,28},{36,32}... | collective-permute-start | bytes 12296 | tf_op jit(solution)/shard_map/ppermute | solution.py:26
  323.4 31.9 %collective-permute-start.22 = (f32[2,136,4]{2,1,0:T(8,128)S(1)}, f32[2,136,4]{2,1,0:T(8,128)S(1)}, u32[]{:S(2)}, u32[]{:S(2)}) collective-permute-start(f32[2,136,4]{2,1,0:T(8,128)S(1)} %get-tuple-element.312), channel_id=1, source_target_pairs={{0,1},{1,2},{2,3},{4,5},{5,6},{6,7},{8,9},{9,10},{10,11},{12,13},{... | collective-permute-start | bytes 13064 | tf_op jit(solution)/shard_map/ppermute | solution.py:23
  353.9 5.6 collective-permute-start.23
  425.0 8.0 %collective-permute-start.24 = (f32[3,4,128]{2,1,0:T(4,128)S(1)}, f32[3,4,128]{2,1,0:T(4,128)S(1)}, u32[]{:S(2)}, u32[]{:S(2)}) collective-permute-start(f32[3,4,128]{2,1,0:T(4,128)S(1)} %get-tuple-element.290), channel_id=1, source_target_pairs={{0,4},{4,8},{8,12},{12,16},{16,20},{20,24},{24,28},{28,32},{32,36}... | collective-permute-start | bytes 18440 | tf_op jit(solution)/shard_map/ppermute | solution.py:23
  430.1 5.5 collective-permute-start.25
  435.7 2.6 collective-permute-start.26
  437.1 4.9 collective-permute-start.27
  442.9 8.0 %collective-permute-start.28 = (f32[2,4,128]{2,1,0:T(4,128)S(1)}, f32[2,4,128]{2,1,0:T(4,128)S(1)}, u32[]{:S(2)}, u32[]{:S(2)}) collective-permute-start(f32[2,4,128]{2,1,0:T(4,128)S(1)} %get-tuple-element.320), channel_id=1, source_target_pairs={{0,4},{4,8},{8,12},{12,16},{16,20},{20,24},{24,28},{28,32},{32,36}... | collective-permute-start | bytes 12296 | tf_op jit(solution)/shard_map/ppermute | solution.py:23
  444.9 7.3 %collective-permute-start.29 = (f32[2,4,128]{2,1,0:T(4,128)S(1)}, f32[2,4,128]{2,1,0:T(4,128)S(1)}, u32[]{:S(2)}, u32[]{:S(2)}) collective-permute-start(f32[2,4,128]{2,1,0:T(4,128)S(1)} %get-tuple-element.321), channel_id=1, source_target_pairs={{4,0},{8,4},{12,8},{16,12},{20,16},{24,20},{28,24},{32,28},{36,32}... | collective-permute-start | bytes 12296 | tf_op jit(solution)/shard_map/ppermute | solution.py:26
  452.3 30.2 %collective-permute-start.30 = (f32[2,136,4]{2,1,0:T(8,128)S(1)}, f32[2,136,4]{2,1,0:T(8,128)S(1)}, u32[]{:S(2)}, u32[]{:S(2)}) collective-permute-start(f32[2,136,4]{2,1,0:T(8,128)S(1)} %get-tuple-element.310), channel_id=1, source_target_pairs={{0,1},{1,2},{2,3},{4,5},{5,6},{6,7},{8,9},{9,10},{10,11},{12,13},{... | collective-permute-start | bytes 13064 | tf_op jit(solution)/shard_map/ppermute | solution.py:23
  481.2 5.6 collective-permute-start.31
  549.7 8.8 %collective-permute-start.32 = (f32[3,4,128]{2,1,0:T(4,128)S(1)}, f32[3,4,128]{2,1,0:T(4,128)S(1)}, u32[]{:S(2)}, u32[]{:S(2)}) collective-permute-start(f32[3,4,128]{2,1,0:T(4,128)S(1)} %get-tuple-element.288), channel_id=1, source_target_pairs={{0,4},{4,8},{8,12},{12,16},{16,20},{20,24},{24,28},{28,32},{32,36}... | collective-permute-start | bytes 18440 | tf_op jit(solution)/shard_map/ppermute | solution.py:23
  556.5 5.5 collective-permute-start.33
  562.2 2.6 collective-permute-start.34
  563.5 4.9 collective-permute-start.35
  569.3 8.0 %collective-permute-start.36 = (f32[2,4,128]{2,1,0:T(4,128)S(1)}, f32[2,4,128]{2,1,0:T(4,128)S(1)}, u32[]{:S(2)}, u32[]{:S(2)}) collective-permute-start(f32[2,4,128]{2,1,0:T(4,128)S(1)} %get-tuple-element.318), channel_id=1, source_target_pairs={{0,4},{4,8},{8,12},{12,16},{16,20},{20,24},{24,28},{28,32},{32,36}... | collective-permute-start | bytes 12296 | tf_op jit(solution)/shard_map/ppermute | solution.py:23
  571.3 7.3 %collective-permute-start.37 = (f32[2,4,128]{2,1,0:T(4,128)S(1)}, f32[2,4,128]{2,1,0:T(4,128)S(1)}, u32[]{:S(2)}, u32[]{:S(2)}) collective-permute-start(f32[2,4,128]{2,1,0:T(4,128)S(1)} %get-tuple-element.319), channel_id=1, source_target_pairs={{4,0},{8,4},{12,8},{16,12},{20,16},{24,20},{28,24},{32,28},{36,32}... | collective-permute-start | bytes 12296 | tf_op jit(solution)/shard_map/ppermute | solution.py:26
  578.7 30.4 %collective-permute-start.38 = (f32[2,136,4]{2,1,0:T(8,128)S(1)}, f32[2,136,4]{2,1,0:T(8,128)S(1)}, u32[]{:S(2)}, u32[]{:S(2)}) collective-permute-start(f32[2,136,4]{2,1,0:T(8,128)S(1)} %get-tuple-element.308), channel_id=1, source_target_pairs={{0,1},{1,2},{2,3},{4,5},{5,6},{6,7},{8,9},{9,10},{10,11},{12,13},{... | collective-permute-start | bytes 13064 | tf_op jit(solution)/shard_map/ppermute | solution.py:23
  607.8 4.8 collective-permute-start.39
where the time goes:
time: 683 us; the launch traced here: 682 us
  blocking collectives  318 us (47%)
  starting transfers between devices  260 us (38%)
  waiting for transfers between devices  79.8 us (12%)
  other arithmetic  11.4 us (2%)
  local copies, waits for them, and re-layouts  8.22 us (1%)
    all_gather x5, blocking collectives, local(): joined = lax.all_gather(block_plane, 'gz', axis=1, tiled=True)  235 us
    ppermute x20, starting transfers between devices, padded_2(): lax.ppermute(lax.slice_in_dim(block, block.shape[dim] - width, None, axis...  200 us
    psum x5, blocking collectives, broadcast(): return lax.psum(kept, axis)  83.9 us
    ppermute x20, waiting for transfers between devices, padded_2(): lax.ppermute(lax.slice_in_dim(block, 0, width, axis=dim), axis, backward)  79.7 us
    ppermute x20, starting transfers between devices, padded_2(): lax.ppermute(lax.slice_in_dim(block, 0, width, axis=dim), axis, backward)  60 us
  transfers between devices with their start and end apart: 40, of which 19 were waited for; matrix products, arithmetic and copies ran while one was open for 0% of the time, Pallas kernels for 0%

commit v1 on v0

v1 whole, which is shorter than its diff:
```python
import functools

import jax
import jax.numpy as jnp
from jax import lax
from jax.experimental import pallas as pl
from jax.experimental.pallas import tpu as pltpu
from jax.sharding import PartitionSpec as P

STEPS = 5
NPD = 8
CELLS = 128
REACH = 8 * STEPS
PAD = 8
OWN = PAD + REACH
HIGH = OWN + CELLS
ROWS = HIGH + REACH + PAD
SPAN = CELLS + 2 * REACH
CHUNK = 16
TAPS = (0.8, -0.2, 4.0 / 105.0, -1.0 / 280.0)
DT = 0.2
MESH = pl.DeviceIdType.MESH


def along_lanes(first, second, lane):
    out = [None, None]
    for m, tap in enumerate(TAPS, 1):
        up = [pltpu.roll(v, CELLS - m, 1) for v in (first, second)]
        down = [pltpu.roll(v, m, 1) for v in (first, second)]
        low, high = lane >= m, lane < CELLS - m
        for t in range(2):
            term = tap * (jnp.where(high, up[t], up[1 - t]) - jnp.where(low, down[t], down[1 - t]))
            out[t] = term if out[t] is None else out[t] + term
    return out


def along_rows(grid, index, start):
    out = []
    for t in range(2):
        total = None
        for m, tap in enumerate(TAPS, 1):
            term = tap * (
                grid[index, t, pl.ds(start + m, CHUNK), :] - grid[index, t, pl.ds(start - m, CHUNK), :]
            )
            total = term if total is None else total + term
        out.append(total)
    return out


def add(a, b):
    return [x + y for x, y in zip(a, b)]


def chunks(low, high, body):
    count = -(-(high - low) // CHUNK)

    def step(i, carry):
        body(pl.multiple_of(low + i * CHUNK, 8))
        return carry

    lax.fori_loop(0, count, step, 0)


def solve(
    sizes, rows_ref, offset_ref, fields_ref, media_ref, out_ref,
    grid, nat, cross, corner, sent_rows, held_rows, chosen,
    halo_send, halo_recv, row_send, row_recv,
):
    n_sec, n_gx, n_gz = sizes
    sec, gx, gz = lax.axis_index("sec"), lax.axis_index("gx"), lax.axis_index("gz")
    is_source = sec == 0
    has_left, has_right = gx > 0, gx < n_gx - 1
    odd = lax.rem(gz, 2) == 1
    sibling = jnp.where(odd, gz - 1, gz + 1)
    crossing = jnp.logical_or(gz == 1, gz == 2)
    partner = 3 - gz

    grid[...] = jnp.zeros_like(grid)
    nat[...] = jnp.zeros_like(nat)
    corner[...] = jnp.zeros_like(corner)

    barrier = pltpu.get_barrier_semaphore()

    def greet(s, x, z):
        pl.semaphore_signal(barrier, inc=1, device_id=(s, x, z), device_id_type=MESH)

    pl.when(has_left)(lambda: greet(sec, gx - 1, gz))
    pl.when(has_right)(lambda: greet(sec, gx + 1, gz))
    greet(sec, gx, sibling)
    pl.when(crossing)(lambda: greet(sec, gx, partner))

    @pl.when(is_source)
    def _():
        for s in range(1, n_sec):
            greet(s, gx, gz)

    pl.when(jnp.logical_not(is_source))(lambda: greet(0, gx, gz))

    for f in range(5):
        grid[f, 0, OWN:HIGH, :] = fields_ref[f].T
    for f in range(3):
        grid[5 + f, 0, OWN:HIGH, :] = media_ref[f].T

    lane1 = lax.broadcasted_iota(jnp.int32, (8, CELLS), 1)
    landing = jnp.full((8, CELLS), -1, jnp.int32)
    offset = offset_ref[jnp.maximum(sec - 1, 0)]
    for k in range(4 * NPD):
        spot = offset + lax.div(rows_ref[k], 2)
        mine = jnp.logical_and(lax.rem(lane1, 4 * NPD) == k, lane1 < 12 * NPD)
        landing = jnp.where(mine, spot, landing)
    depth = lax.broadcasted_iota(jnp.int32, (SPAN, CELLS), 0) + (gz * CELLS - REACH)
    hit = depth == jnp.broadcast_to(landing[0:1], (SPAN, CELLS))
    chosen[...] = jnp.where(hit, 0.5, 0.0).astype(jnp.bfloat16)

    waits = (
        1
        + has_left.astype(jnp.int32)
        + has_right.astype(jnp.int32)
        + crossing.astype(jnp.int32)
        + jnp.where(is_source, n_sec - 1, 1)
    )
    pl.semaphore_wait(barrier, waits)

    def remote(src, dst, i, where):
        return pltpu.make_async_remote_copy(
            src, dst, halo_send.at[i], halo_recv.at[i], device_id=where, device_id_type=MESH
        )

    left, right = (sec, gx - 1, gz), (sec, gx + 1, gz)
    over = (sec, gx, partner)
    near = (sec, gx, sibling)
    cross_from = pl.multiple_of(jnp.where(gz == 1, HIGH - REACH, OWN), 8)
    cross_to = pl.multiple_of(jnp.where(gz == 1, HIGH, PAD), 8)
    near_from = pl.multiple_of(jnp.where(odd, OWN, HIGH - REACH), 8)
    near_to = pl.multiple_of(jnp.where(odd, HIGH, PAD), 8)

    over_copy = remote(grid.at[:, 0, pl.ds(cross_from, REACH), :], cross, 0, over)
    pl.when(crossing)(over_copy.start)

    edge = CELLS - REACH
    left_copies = [
        remote(fields_ref.at[:, 0:REACH, :], nat.at[0:5, 0:REACH, :], 1, left),
        remote(media_ref.at[:, 0:REACH, :], nat.at[5:8, 0:REACH, :], 2, left),
    ]
    right_copies = [
        remote(fields_ref.at[:, edge:CELLS, :], nat.at[0:5, edge:CELLS, :], 3, right),
        remote(media_ref.at[:, edge:CELLS, :], nat.at[5:8, edge:CELLS, :], 4, right),
    ]

    def each(copies, name):
        def run():
            for c in copies:
                getattr(c, name)()

        return run

    pl.when(has_left)(each(left_copies, "start"))
    pl.when(has_right)(each(right_copies, "start"))
    pl.when(has_right)(each(left_copies, "wait_recv"))
    pl.when(has_left)(each(right_copies, "wait_recv"))
    for f in range(8):
        grid[f, 1, OWN:HIGH, :] = nat[f].T

    near_copy = remote(
        grid.at[:, :, pl.ds(near_from, REACH), :], grid.at[:, :, pl.ds(near_to, REACH), :], 5, near
    )
    near_copy.start()

    corner_left = remote(cross, corner.at[0], 6, left)
    corner_right = remote(cross, corner.at[1], 7, right)

    @pl.when(crossing)
    def _():
        over_copy.wait_recv()
        pl.when(has_left)(corner_left.start)
        pl.when(has_right)(corner_right.start)
        lanes = lax.broadcasted_iota(jnp.int32, (REACH, CELLS), 1)
        for f in range(8):
            grid[f, 0, pl.ds(cross_to, REACH), :] = cross[f]
        pl.when(has_right)(corner_left.wait_recv)
        pl.when(has_left)(corner_right.wait_recv)
        for f in range(8):
            joined = jnp.where(lanes < REACH, corner[0, f], jnp.where(lanes >= edge, corner[1, f], 0.0))
            grid[f, 1, pl.ds(cross_to, REACH), :] = joined

    near_copy.wait()
    pl.when(crossing)(over_copy.wait_send)

    lane = lax.broadcasted_iota(jnp.int32, (CHUNK, CELLS), 1)

    def get(f, start):
        return [grid[f, t, pl.ds(start, CHUNK), :] for t in range(2)]

    def put(f, start, values):
        for t in range(2):
            grid[f, t, pl.ds(start, CHUNK), :] = values[t]

    def row_copy(i, step, where):
        return pltpu.make_async_remote_copy(
            sent_rows.at[step], held_rows.at[step, gz], row_send.at[i, step], row_recv.at[0, step],
            device_id=where, device_id_type=MESH,
        )

    @pl.when(is_source)
    def _():
        for step in range(STEPS):
            reach = 8 * (STEPS - step)

            def velocities(start):
                buoyancy = get(5, start)
                shear = get(4, start)
                force_x = add(along_lanes(*get(2, start), lane), along_rows(grid, 4, start))
                force_z = add(along_lanes(*shear, lane), along_rows(grid, 3, start))
                put(0, start, [v + DT * b * g for v, b, g in zip(get(0, start), buoyancy, force_x)])
                put(1, start, [v + DT * b * g for v, b, g in zip(get(1, start), buoyancy, force_z)])

            def stresses(start):
                first, second = get(6, start), get(7, start)
                vx, vz = get(0, start), get(1, start)
                strain_x, strain_z = along_lanes(*vx, lane), along_rows(grid, 1, start)
                bend = add(along_rows(grid, 0, start), along_lanes(*vz, lane))
                xx, zz, xz = get(2, start), get(3, start), get(4, start)
                for t in range(2):
                    stiff = first[t] + 2.0 * second[t]
                    xx[t] = xx[t] + DT * (stiff * strain_x[t] + first[t] * strain_z[t])
                    zz[t] = zz[t] + DT * (first[t] * strain_x[t] + stiff * strain_z[t])
                    xz[t] = xz[t] + DT * second[t] * bend[t]
                put(2, start, xx)
                put(3, start, zz)
                put(4, start, xz)

            chunks(OWN - reach, HIGH + reach, velocities)
            chunks(OWN - reach + 8, HIGH + reach - 8, stresses)
            for k in range(NPD):
                row = lax.rem(rows_ref[gz * NPD + k], CELLS) + OWN
                for t in range(2):
                    line = [grid[f, t, pl.ds(row, 1), :] for f in range(4)]
                    sent_rows[step, 0, t, k : k + 1, :] = line[0]
                    sent_rows[step, 1, t, k : k + 1, :] = line[1]
                    sent_rows[step, 2, t, k : k + 1, :] = -0.5 * (line[2] + line[3])
            for s in range(1, n_sec):
                row_copy(s - 1, step, (s, gx, gz)).start()
        for step in range(STEPS):
            for s in range(1, n_sec):
                row_copy(s - 1, step, (s, gx, gz)).wait_send()

    @pl.when(jnp.logical_not(is_source))
    def _():
        half = lax.div(gz, 2) * 2
        other = 2 - half

        def hand_on(i, step, blocks, where):
            return pltpu.make_async_remote_copy(
                held_rows.at[step, blocks], held_rows.at[step, blocks], row_send.at[i - 1, step],
                row_recv.at[i, step], device_id=where, device_id_type=MESH,
            )

        def to_sibling(step):
            return hand_on(1, step, pl.ds(gz, 1), near)

        def from_sibling(step):
            return hand_on(1, step, pl.ds(sibling, 1), near)

        def to_partner(step):
            return hand_on(2, step, pl.ds(half, 2), over)

        def from_partner(step):
            return hand_on(2, step, pl.ds(other, 2), over)

        def to_rest(step):
            return hand_on(3, step, pl.ds(other, 2), near)

        def velocities(start):
            buoyancy = get(5, start)
            slope_x = along_lanes(*get(2, start), lane)
            slope_z = along_rows(grid, 2, start)
            put(0, start, [v - DT * b * g for v, b, g in zip(get(0, start), buoyancy, slope_x)])
            put(1, start, [v - DT * b * g for v, b, g in zip(get(1, start), buoyancy, slope_z)])

        def pressures(start):
            kappa, strength = get(6, start), get(7, start)
            spread = add(along_lanes(*get(0, start), lane), along_rows(grid, 1, start))
            p, one, two = get(2, start), get(3, start), get(4, start)
            for t in range(2):
                load = kappa[t] * spread[t]
                driven = strength[t] * load
                one[t] = 0.9 * one[t] + (1.0 - 0.9) * 0.15 * driven
                two[t] = 0.5 * two[t] + (1.0 - 0.5) * 0.1 * driven
                p[t] = p[t] - DT * (load - one[t] - two[t])
            put(2, start, p)
            put(3, start, one)
            put(4, start, two)

        def evolve(step):
            reach = 8 * (STEPS - step)
            chunks(OWN - reach, HIGH + reach, velocities)
            chunks(OWN - reach + 8, HIGH + reach - 8, pressures)

        evolve(0)
        for step in range(STEPS):
            row_copy(0, step, near).wait_recv()
            to_sibling(step).start()

            @pl.when(crossing)
            def _():
                from_sibling(step).wait_recv()
                to_partner(step).start()

        for step in range(STEPS):
            pl.when(jnp.logical_not(crossing))(from_sibling(step).wait_recv)

            @pl.when(crossing)
            def _():
                from_partner(step).wait_recv()
                to_rest(step).start()

            pl.when(jnp.logical_not(crossing))(to_rest(step).wait_recv)
            low = OWN - 8 * (STEPS - 1 - step)
            high = HIGH + 8 * (STEPS - 1 - step)
            pick = chosen[low - PAD : high - PAD, :]
            for c in range(3):
                for t in range(2 if step < STEPS - 1 else 1):
                    lines = held_rows[step, :, c, t].reshape(4 * NPD, CELLS)
                    top = lines.astype(jnp.bfloat16)
                    rest = lines - top.astype(jnp.float32)
                    mid = rest.astype(jnp.bfloat16)
                    last = (rest - mid.astype(jnp.float32)).astype(jnp.bfloat16)
                    stack = jnp.concatenate([top, mid, last, jnp.zeros_like(top)], axis=0)
                    grid[c, t, low:high, :] += jnp.dot(pick, stack, preferred_element_type=jnp.float32)
            if step < STEPS - 1:
                evolve(step + 1)

        for step in range(STEPS):
            to_sibling(step).wait_send()

            @pl.when(crossing)
            def _():
                to_partner(step).wait_send()
                to_rest(step).wait_send()

    for f in range(5):
        out_ref[f] = grid[f, 0, OWN:HIGH, :].T

    pl.when(has_left)(each(left_copies, "wait_send"))
    pl.when(has_right)(each(right_copies, "wait_send"))

    @pl.when(crossing)
    def _():
        pl.when(has_left)(corner_left.wait_send)
        pl.when(has_right)(corner_right.wait_send)


def solution(mesh):
    sizes = tuple(mesh.shape[a] for a in ("sec", "gx", "gz"))

    def local(fields, media, plane_rows, box_offset):
        vmem = pl.BlockSpec(memory_space=pltpu.VMEM)
        smem = pl.BlockSpec(memory_space=pltpu.SMEM)
        out = pl.pallas_call(
            functools.partial(solve, sizes),
            out_shape=jax.ShapeDtypeStruct((5, CELLS, CELLS), jnp.float32),
            in_specs=[smem, smem, vmem, vmem],
            out_specs=vmem,
            scratch_shapes=[
                pltpu.VMEM((8, 2, ROWS, CELLS), jnp.float32),
                pltpu.VMEM((8, CELLS, CELLS), jnp.float32),
                pltpu.VMEM((8, REACH, CELLS), jnp.float32),
                pltpu.VMEM((2, 8, REACH, CELLS), jnp.float32),
                pltpu.VMEM((STEPS, 3, 2, NPD, CELLS), jnp.float32),
                pltpu.VMEM((STEPS, 4, 3, 2, NPD, CELLS), jnp.float32),
                pltpu.VMEM((SPAN, CELLS), jnp.bfloat16),
                pltpu.SemaphoreType.DMA((8,)),
                pltpu.SemaphoreType.DMA((8,)),
                pltpu.SemaphoreType.DMA((3, STEPS)),
                pltpu.SemaphoreType.DMA((4, STEPS)),
            ],
            compiler_params=pltpu.CompilerParams(collective_id=0, has_side_effects=True),
        )(plane_rows, box_offset, fields[0], media[0])
        return out[None]

    spec = P("sec", None, "gx", "gz")
    return jax.shard_map(
        local, mesh=mesh, in_specs=(spec, spec, P(), P()), out_specs=spec, check_vma=False
    )
```

time: 683 us -> 98.1 us (0.14)
  the two profiles are of different devices: /device:TPU:32 before, /device:TPU:7 now
where the time goes in v1:
time: 98.1 us; the launch traced here: 97.9 us
  Pallas kernels  96.2 us (98%)
  local copies, waits for them, and re-layouts  1.72 us (2%)
    pallas_call x1, Pallas kernels, local(): pl.pallas_call(functools.partial(solve, sizes), out_shape=jax.ShapeDtypeS...  96.2 us

profile of v1, /device:TPU:7, one launch (start us, length us, event | category | flops | bytes accessed | tf_op | source)
XLA Modules:
  0.0 97.9 jit_solution(848858218771596245)
XLA Ops:
  0.0 96.2 %shard_map.46 = f32[5,128,128]{2,1,0:T(8,128)} custom-call(s32[32]{0:T(128)} %rows_ref.1, s32[3]{0:T(128)} %offset_ref.1, f32[5,128,128]{2,1,0:T(8,128)} %bitcast.4, f32[3,128,128]{2,1,0:T(8,128)} %bitcast.5), custom_call_target="tpu_custom_call" | custom-call | tf_op jit(solution)/shard_map/pallas_call | solution.py:359
  96.2 1.7 %copy.6 = f32[1,5,128,128]{3,2,1,0:T(8,128)} copy(f32[1,5,128,128]{3,2,1,0:T(8,128)} %bitcast.3) | data formatting | bytes 655360

commit v2 on v1

--- a/solution.py
+++ b/solution.py
@@ -51,14 +51,20 @@
     return [x + y for x, y in zip(a, b)]
 
 
-def chunks(low, high, body):
-    count = -(-(high - low) // CHUNK)
+def chunks(low, high, body, save):
+    count = (high - low) // CHUNK
 
     def step(i, carry):
-        body(pl.multiple_of(low + i * CHUNK, 8))
+        starts = [pl.multiple_of(low + (2 * i + j) * CHUNK, 8) for j in range(2)]
+        results = [body(start) for start in starts]
+        for start, result in zip(starts, results):
+            save(start, result)
         return carry
 
-    lax.fori_loop(0, count, step, 0)
+    lax.fori_loop(0, count // 2, step, 0)
+    if count % 2:
+        start = low + (count - 1) * CHUNK
+        save(start, body(start))
 
 
 def solve(
@@ -94,7 +100,14 @@
         for s in range(1, n_sec):
             greet(s, gx, gz)
 
-    pl.when(jnp.logical_not(is_source))(lambda: greet(0, gx, gz))
+    @pl.when(jnp.logical_not(is_source))
+    def _():
+        greet(0, gx, gz)
+        for o in range(1, n_sec - 1):
+            s = 1 + lax.rem(sec - 1 + o, n_sec - 1)
+            greet(s, gx, gz)
+            greet(s, gx, sibling)
+
 
     for f in range(5):
         grid[f, 0, OWN:HIGH, :] = fields_ref[f].T
@@ -117,7 +130,7 @@
         + has_left.astype(jnp.int32)
         + has_right.astype(jnp.int32)
         + crossing.astype(jnp.int32)
-        + jnp.where(is_source, n_sec - 1, 1)
+        + jnp.where(is_source, n_sec - 1, 1 + 2 * (n_sec - 2))
     )
     pl.semaphore_wait(barrier, waits)
 
@@ -191,13 +204,17 @@
     def get(f, start):
         return [grid[f, t, pl.ds(start, CHUNK), :] for t in range(2)]
 
-    def put(f, start, values):
-        for t in range(2):
-            grid[f, t, pl.ds(start, CHUNK), :] = values[t]
+    def save(start, fields):
+        for f, values in fields.items():
+            for t in range(2):
+                grid[f, t, pl.ds(start, CHUNK), :] = values[t]
+
+    def tiles(step):
+        return pl.ds(0, 2 if step < STEPS - 1 else 1)
 
     def row_copy(i, step, where):
         return pltpu.make_async_remote_copy(
-            sent_rows.at[step], held_rows.at[step, gz], row_send.at[i, step], row_recv.at[0, step],
+            sent_rows.at[step, tiles(step)], held_rows.at[step, tiles(step), gz], row_send.at[i, step], row_recv.at[0, step],
             device_id=where, device_id_type=MESH,
         )
 
@@ -211,8 +228,10 @@
                 shear = get(4, start)
                 force_x = add(along_lanes(*get(2, start), lane), along_rows(grid, 4, start))
                 force_z = add(along_lanes(*shear, lane), along_rows(grid, 3, start))
-                put(0, start, [v + DT * b * g for v, b, g in zip(get(0, start), buoyancy, force_x)])
-                put(1, start, [v + DT * b * g for v, b, g in zip(get(1, start), buoyancy, force_z)])
+                return {
+                    0: [v + DT * b * g for v, b, g in zip(get(0, start), buoyancy, force_x)],
+                    1: [v + DT * b * g for v, b, g in zip(get(1, start), buoyancy, force_z)],
+                }
 
             def stresses(start):
                 first, second = get(6, start), get(7, start)
@@ -225,19 +244,17 @@
                     xx[t] = xx[t] + DT * (stiff * strain_x[t] + first[t] * strain_z[t])
                     zz[t] = zz[t] + DT * (first[t] * strain_x[t] + stiff * strain_z[t])
                     xz[t] = xz[t] + DT * second[t] * bend[t]
-                put(2, start, xx)
-                put(3, start, zz)
-                put(4, start, xz)
-
-            chunks(OWN - reach, HIGH + reach, velocities)
-            chunks(OWN - reach + 8, HIGH + reach - 8, stresses)
+                return {2: xx, 3: zz, 4: xz}
+
+            chunks(OWN - reach, HIGH + reach, velocities, save)
+            chunks(OWN - reach + 8, HIGH + reach - 8, stresses, save)
             for k in range(NPD):
                 row = lax.rem(rows_ref[gz * NPD + k], CELLS) + OWN
                 for t in range(2):
                     line = [grid[f, t, pl.ds(row, 1), :] for f in range(4)]
-                    sent_rows[step, 0, t, k : k + 1, :] = line[0]
-                    sent_rows[step, 1, t, k : k + 1, :] = line[1]
-                    sent_rows[step, 2, t, k : k + 1, :] = -0.5 * (line[2] + line[3])
+                    sent_rows[step, t, 0, k : k + 1, :] = line[0]
+                    sent_rows[step, t, 1, k : k + 1, :] = line[1]
+                    sent_rows[step, t, 2, k : k + 1, :] = -0.5 * (line[2] + line[3])
             for s in range(1, n_sec):
                 row_copy(s - 1, step, (s, gx, gz)).start()
         for step in range(STEPS):
@@ -249,33 +266,61 @@
         half = lax.div(gz, 2) * 2
         other = 2 - half
 
-        def hand_on(i, step, blocks, where):
+        part = sec - 1
+        others = [lax.rem(part + 1, 3), lax.rem(part + 2, 3)]
+
+        def hand_on(i, step, blocks, parts, where):
+            piece = held_rows.at[step, tiles(step), blocks, parts]
             return pltpu.make_async_remote_copy(
-                held_rows.at[step, blocks], held_rows.at[step, blocks], row_send.at[i - 1, step],
-                row_recv.at[i, step], device_id=where, device_id_type=MESH,
+                piece, piece, row_send.at[i, step], row_recv.at[i, step], device_id=where, device_id_type=MESH
             )
 
+        whole = pl.ds(0, 3)
+
         def to_sibling(step):
-            return hand_on(1, step, pl.ds(gz, 1), near)
+            return hand_on(1, step, pl.ds(gz, 1), whole, near)
 
         def from_sibling(step):
-            return hand_on(1, step, pl.ds(sibling, 1), near)
+            return hand_on(1, step, pl.ds(sibling, 1), whole, near)
 
         def to_partner(step):
-            return hand_on(2, step, pl.ds(half, 2), over)
+            return hand_on(2, step, pl.ds(gz, 1), pl.ds(part, 1), over)
 
         def from_partner(step):
-            return hand_on(2, step, pl.ds(other, 2), over)
-
-        def to_rest(step):
-            return hand_on(3, step, pl.ds(other, 2), near)
+            return hand_on(2, step, pl.ds(partner, 1), pl.ds(part, 1), over)
+
+        def nearby_to_partner(step):
+            return hand_on(3, step, pl.ds(sibling, 1), pl.ds(part, 1), over)
+
+        def nearby_from_partner(step):
+            return hand_on(3, step, pl.ds(3 - sibling, 1), pl.ds(part, 1), over)
+
+        def spread(step):
+            piece = held_rows.at[step, tiles(step), pl.ds(other, 2), pl.ds(part, 1)]
+            places = [near] + [(1 + o, gx, z) for o in others for z in (gz, sibling)]
+            return [
+                pltpu.make_async_remote_copy(
+                    piece, piece, row_send.at[i, step], row_recv.at[4 + part, step],
+                    device_id=place, device_id_type=MESH,
+                )
+                for i, place in zip((0, 4, 5, 6, 7), places)
+            ]
+
+        def spread_in(step, which):
+            piece = held_rows.at[step, tiles(step), pl.ds(other, 2), pl.ds(which, 1)]
+            return pltpu.make_async_remote_copy(
+                piece, piece, row_send.at[0, step], row_recv.at[4 + which, step],
+                device_id=near, device_id_type=MESH,
+            )
 
         def velocities(start):
             buoyancy = get(5, start)
             slope_x = along_lanes(*get(2, start), lane)
             slope_z = along_rows(grid, 2, start)
-            put(0, start, [v - DT * b * g for v, b, g in zip(get(0, start), buoyancy, slope_x)])
-            put(1, start, [v - DT * b * g for v, b, g in zip(get(1, start), buoyancy, slope_z)])
+            return {
+                0: [v - DT * b * g for v, b, g in zip(get(0, start), buoyancy, slope_x)],
+                1: [v - DT * b * g for v, b, g in zip(get(1, start), buoyancy, slope_z)],
+            }
 
         def pressures(start):
             kappa, strength = get(6, start), get(7, start)
@@ -287,40 +332,48 @@
                 one[t] = 0.9 * one[t] + (1.0 - 0.9) * 0.15 * driven
                 two[t] = 0.5 * two[t] + (1.0 - 0.5) * 0.1 * driven
                 p[t] = p[t] - DT * (load - one[t] - two[t])
-            put(2, start, p)
-            put(3, start, one)
-            put(4, start, two)
+            return {2: p, 3: one, 4: two}
 
         def evolve(step):
             reach = 8 * (STEPS - step)
-            chunks(OWN - reach, HIGH + reach, velocities)
-            chunks(OWN - reach + 8, HIGH + reach - 8, pressures)
+            chunks(OWN - reach, HIGH + reach, velocities, save)
+            chunks(OWN - reach + 8, HIGH + reach - 8, pressures, save)
 
         evolve(0)
+
+        @pl.when(crossing)
+        def _():
+            for step in range(STEPS):
+                from_sibling(step).wait_recv()
+                nearby_to_partner(step).start()
+
         for step in range(STEPS):
             row_copy(0, step, near).wait_recv()
+            pl.when(crossing)(to_partner(step).start)
             to_sibling(step).start()
 
+        def pass_on(step):
             @pl.when(crossing)
             def _():
-                from_sibling(step).wait_recv()
-                to_partner(step).start()
-
+                nearby_from_partner(step).wait_recv()
+                from_partner(step).wait_recv()
+                for c in spread(step):
+                    c.start()
+
+        pass_on(0)
         for step in range(STEPS):
+            if step < STEPS - 1:
+                pass_on(step + 1)
             pl.when(jnp.logical_not(crossing))(from_sibling(step).wait_recv)
-
-            @pl.when(crossing)
-            def _():
-                from_partner(step).wait_recv()
-                to_rest(step).start()
-
-            pl.when(jnp.logical_not(crossing))(to_rest(step).wait_recv)
+            for which in others:
+                spread_in(step, which).wait_recv()
+            pl.when(jnp.logical_not(crossing))(spread_in(step, part).wait_recv)
             low = OWN - 8 * (STEPS - 1 - step)
             high = HIGH + 8 * (STEPS - 1 - step)
             pick = chosen[low - PAD : high - PAD, :]
             for c in range(3):
                 for t in range(2 if step < STEPS - 1 else 1):
-                    lines = held_rows[step, :, c, t].reshape(4 * NPD, CELLS)
+                    lines = held_rows[step, t, :, c].reshape(4 * NPD, CELLS)
                     top = lines.astype(jnp.bfloat16)
                     rest = lines - top.astype(jnp.float32)
                     mid = rest.astype(jnp.bfloat16)
@@ -336,7 +389,9 @@
             @pl.when(crossing)
             def _():
                 to_partner(step).wait_send()
-                to_rest(step).wait_send()
+                nearby_to_partner(step).wait_send()
+                for c in spread(step):
+                    c.wait_send()
 
     for f in range(5):
         out_ref[f] = grid[f, 0, OWN:HIGH, :].T
@@ -366,13 +421,13 @@
                 pltpu.VMEM((8, CELLS, CELLS), jnp.float32),
                 pltpu.VMEM((8, REACH, CELLS), jnp.float32),
                 pltpu.VMEM((2, 8, REACH, CELLS), jnp.float32),
-                pltpu.VMEM((STEPS, 3, 2, NPD, CELLS), jnp.float32),
-                pltpu.VMEM((STEPS, 4, 3, 2, NPD, CELLS), jnp.float32),
+                pltpu.VMEM((STEPS, 2, 3, NPD, CELLS), jnp.float32),
+                pltpu.VMEM((STEPS, 2, 4, 3, NPD, CELLS), jnp.float32),
                 pltpu.VMEM((SPAN, CELLS), jnp.bfloat16),
                 pltpu.SemaphoreType.DMA((8,)),
                 pltpu.SemaphoreType.DMA((8,)),
-                pltpu.SemaphoreType.DMA((3, STEPS)),
-                pltpu.SemaphoreType.DMA((4, STEPS)),
+                pltpu.SemaphoreType.DMA((8, STEPS)),
+                pltpu.SemaphoreType.DMA((8, STEPS)),
             ],
             compiler_params=pltpu.CompilerParams(collective_id=0, has_side_effects=True),
         )(plane_rows, box_offset, fields[0], media[0])

time: 98.1 us -> 84.5 us (0.86)
  the two profiles are of different devices: /device:TPU:7 before, /device:TPU:98 now
where the time goes in v2:
time: 84.5 us; the launch traced here: 84.3 us
  Pallas kernels  82.5 us (98%)
  local copies, waits for them, and re-layouts  1.72 us (2%)
    pallas_call x1, Pallas kernels, local(): pl.pallas_call(functools.partial(solve, sizes), out_shape=jax.ShapeDtypeS...  82.5 us
    unnamed x1, local copies, waits for them, and re-layouts  1.72 us

profile of v2, /device:TPU:98, one launch (start us, length us, event | category | flops | bytes accessed | tf_op | source)
XLA Modules:
  0.0 84.3 jit_solution(5821917282415516678)
XLA Ops:
  0.0 82.5 %shard_map.46 = f32[5,128,128]{2,1,0:T(8,128)} custom-call(s32[32]{0:T(128)} %rows_ref.1, s32[3]{0:T(128)} %offset_ref.1, f32[5,128,128]{2,1,0:T(8,128)} %bitcast.4, f32[3,128,128]{2,1,0:T(8,128)} %bitcast.5), custom_call_target="tpu_custom_call" | custom-call | tf_op jit(solution)/shard_map/pallas_call | solution.py:414
  82.5 1.7 %copy.6 = f32[1,5,128,128]{3,2,1,0:T(8,128)} copy(f32[1,5,128,128]{3,2,1,0:T(8,128)} %bitcast.3) | data formatting | bytes 655360

commit v3 on v2

--- a/solution.py
+++ b/solution.py
@@ -78,22 +78,31 @@
     has_left, has_right = gx > 0, gx < n_gx - 1
     odd = lax.rem(gz, 2) == 1
     sibling = jnp.where(odd, gz - 1, gz + 1)
-    crossing = jnp.logical_or(gz == 1, gz == 2)
+    lower, upper = gz == 1, gz == 2
+    crossing = jnp.logical_or(lower, upper)
     partner = 3 - gz
 
+    barrier = pltpu.get_barrier_semaphore()
+
+    def greet(s, x, z):
+        pl.semaphore_signal(barrier, inc=1, device_id=(s, x, z), device_id_type=MESH)
+
+    cross[...] = jnp.zeros_like(cross)
+    pl.when(crossing)(lambda: greet(sec, gx, partner))
     grid[...] = jnp.zeros_like(grid)
     nat[...] = jnp.zeros_like(nat)
-    corner[...] = jnp.zeros_like(corner)
-
-    barrier = pltpu.get_barrier_semaphore()
-
-    def greet(s, x, z):
-        pl.semaphore_signal(barrier, inc=1, device_id=(s, x, z), device_id_type=MESH)
+
+    @pl.when(jnp.logical_not(has_right))
+    def _():
+        corner[0] = jnp.zeros_like(corner[0])
+
+    @pl.when(jnp.logical_not(has_left))
+    def _():
+        corner[1] = jnp.zeros_like(corner[1])
 
     pl.when(has_left)(lambda: greet(sec, gx - 1, gz))
     pl.when(has_right)(lambda: greet(sec, gx + 1, gz))
     greet(sec, gx, sibling)
-    pl.when(crossing)(lambda: greet(sec, gx, partner))
 
     @pl.when(is_source)
     def _():
@@ -142,22 +151,18 @@
     left, right = (sec, gx - 1, gz), (sec, gx + 1, gz)
     over = (sec, gx, partner)
     near = (sec, gx, sibling)
-    cross_from = pl.multiple_of(jnp.where(gz == 1, HIGH - REACH, OWN), 8)
     cross_to = pl.multiple_of(jnp.where(gz == 1, HIGH, PAD), 8)
     near_from = pl.multiple_of(jnp.where(odd, OWN, HIGH - REACH), 8)
     near_to = pl.multiple_of(jnp.where(odd, HIGH, PAD), 8)
 
-    over_copy = remote(grid.at[:, 0, pl.ds(cross_from, REACH), :], cross, 0, over)
-    pl.when(crossing)(over_copy.start)
-
     edge = CELLS - REACH
     left_copies = [
-        remote(fields_ref.at[:, 0:REACH, :], nat.at[0:5, 0:REACH, :], 1, left),
-        remote(media_ref.at[:, 0:REACH, :], nat.at[5:8, 0:REACH, :], 2, left),
+        remote(fields_ref.at[:, 0:REACH, :], nat.at[0:5, 0:REACH, :], 24, left),
+        remote(media_ref.at[:, 0:REACH, :], nat.at[5:8, 0:REACH, :], 25, left),
     ]
     right_copies = [
-        remote(fields_ref.at[:, edge:CELLS, :], nat.at[0:5, edge:CELLS, :], 3, right),
-        remote(media_ref.at[:, edge:CELLS, :], nat.at[5:8, edge:CELLS, :], 4, right),
+        remote(fields_ref.at[:, edge:CELLS, :], nat.at[0:5, edge:CELLS, :], 26, right),
+        remote(media_ref.at[:, edge:CELLS, :], nat.at[5:8, edge:CELLS, :], 27, right),
     ]
 
     def each(copies, name):
@@ -167,37 +172,82 @@
 
         return run
 
+    deep = {0: 40, 1: 40, 2: 40, 3: 40, 4: 40, 5: 40, 6: 32, 7: 32}
+    flat = {0: 32, 1: 40, 2: 40, 3: 32, 4: 32, 5: 40, 6: 32, 7: 32}
+
+    def depths(f, act):
+        if deep[f] == flat[f]:
+            act(deep[f])
+        else:
+            pl.when(is_source)(lambda: act(deep[f]))
+            pl.when(jnp.logical_not(is_source))(lambda: act(flat[f]))
+
+    def over_copy(f, depth, low):
+        if low:
+            src, dst = grid.at[f, 0, HIGH - depth : HIGH, :], cross.at[f, REACH - depth : REACH, :]
+        else:
+            src, dst = grid.at[f, 0, OWN : OWN + depth, :], cross.at[f, 0:depth, :]
+        return remote(src, dst, f, over)
+
+    def corner_copy(f, depth, low, side):
+        rows = pl.ds(0, depth) if low else pl.ds(REACH - depth, depth)
+        place = left if side == 0 else right
+        return remote(cross.at[f, rows, :], corner.at[side, f, rows, :], 8 + 8 * side + f, place)
+
+    def over_start(low):
+        for f in range(8):
+            depths(f, lambda depth: over_copy(f, depth, low).start())
+
+    pl.when(upper)(lambda: over_start(False))
+    pl.when(lower)(lambda: over_start(True))
     pl.when(has_left)(each(left_copies, "start"))
     pl.when(has_right)(each(right_copies, "start"))
+
+
     pl.when(has_right)(each(left_copies, "wait_recv"))
     pl.when(has_left)(each(right_copies, "wait_recv"))
     for f in range(8):
         grid[f, 1, OWN:HIGH, :] = nat[f].T
 
     near_copy = remote(
-        grid.at[:, :, pl.ds(near_from, REACH), :], grid.at[:, :, pl.ds(near_to, REACH), :], 5, near
+        grid.at[:, :, pl.ds(near_from, REACH), :], grid.at[:, :, pl.ds(near_to, REACH), :], 28, near
     )
     near_copy.start()
 
-    corner_left = remote(cross, corner.at[0], 6, left)
-    corner_right = remote(cross, corner.at[1], 7, right)
-
-    @pl.when(crossing)
-    def _():
-        over_copy.wait_recv()
-        pl.when(has_left)(corner_left.start)
-        pl.when(has_right)(corner_right.start)
-        lanes = lax.broadcasted_iota(jnp.int32, (REACH, CELLS), 1)
+    lanes = lax.broadcasted_iota(jnp.int32, (REACH, CELLS), 1)
+
+    def take_halo(low):
         for f in range(8):
+
+            def arrive(depth):
+                over_copy(f, depth, not low).wait_recv()
+                pl.when(has_left)(corner_copy(f, depth, low, 0).start)
+                pl.when(has_right)(corner_copy(f, depth, low, 1).start)
+
+            depths(f, arrive)
             grid[f, 0, pl.ds(cross_to, REACH), :] = cross[f]
-        pl.when(has_right)(corner_left.wait_recv)
-        pl.when(has_left)(corner_right.wait_recv)
         for f in range(8):
+
+            def arrive(depth):
+                pl.when(has_right)(corner_copy(f, depth, low, 0).wait_recv)
+                pl.when(has_left)(corner_copy(f, depth, low, 1).wait_recv)
+
+            depths(f, arrive)
             joined = jnp.where(lanes < REACH, corner[0, f], jnp.where(lanes >= edge, corner[1, f], 0.0))
             grid[f, 1, pl.ds(cross_to, REACH), :] = joined
 
+        for f in range(8):
+
+            def leave(depth):
+                over_copy(f, depth, low).wait_send()
+                pl.when(has_left)(corner_copy(f, depth, low, 0).wait_send)
+                pl.when(has_right)(corner_copy(f, depth, low, 1).wait_send)
+
+            depths(f, leave)
+
+    pl.when(lower)(lambda: take_halo(True))
+    pl.when(upper)(lambda: take_halo(False))
     near_copy.wait()
-    pl.when(crossing)(over_copy.wait_send)
 
     lane = lax.broadcasted_iota(jnp.int32, (CHUNK, CELLS), 1)
 
@@ -206,8 +256,8 @@
 
     def save(start, fields):
         for f, values in fields.items():
-            for t in range(2):
-                grid[f, t, pl.ds(start, CHUNK), :] = values[t]
+            for t, value in enumerate(values):
+                grid[f, t, pl.ds(start, CHUNK), :] = value
 
     def tiles(step):
         return pl.ds(0, 2 if step < STEPS - 1 else 1)
@@ -216,6 +266,17 @@
         return pltpu.make_async_remote_copy(
             sent_rows.at[step, tiles(step)], held_rows.at[step, tiles(step), gz], row_send.at[i, step], row_recv.at[0, step],
             device_id=where, device_id_type=MESH,
+        )
+
+    def crossed(step, part):
+        return pl.ds(part, 1) if step < STEPS - 1 else pl.ds(0, 3)
+
+    def row_over(step, s):
+        parts = crossed(step, s - 1)
+        return pltpu.make_async_remote_copy(
+            sent_rows.at[step, tiles(step), parts], held_rows.at[step, tiles(step), gz, parts],
+            row_send.at[2 + s, step], row_recv.at[2, step],
+            device_id=(s, gx, partner), device_id_type=MESH,
         )
 
     @pl.when(is_source)
@@ -234,12 +295,13 @@
                 }
 
             def stresses(start):
+                count = 2 if step < STEPS - 1 else 1
                 first, second = get(6, start), get(7, start)
                 vx, vz = get(0, start), get(1, start)
                 strain_x, strain_z = along_lanes(*vx, lane), along_rows(grid, 1, start)
                 bend = add(along_rows(grid, 0, start), along_lanes(*vz, lane))
-                xx, zz, xz = get(2, start), get(3, start), get(4, start)
-                for t in range(2):
+                xx, zz, xz = (get(f, start)[:count] for f in (2, 3, 4))
+                for t in range(count):
                     stiff = first[t] + 2.0 * second[t]
                     xx[t] = xx[t] + DT * (stiff * strain_x[t] + first[t] * strain_z[t])
                     zz[t] = zz[t] + DT * (first[t] * strain_x[t] + stiff * strain_z[t])
@@ -255,11 +317,18 @@
                     sent_rows[step, t, 0, k : k + 1, :] = line[0]
                     sent_rows[step, t, 1, k : k + 1, :] = line[1]
                     sent_rows[step, t, 2, k : k + 1, :] = -0.5 * (line[2] + line[3])
+
+            @pl.when(crossing)
+            def _():
+                for s in range(1, n_sec):
+                    row_over(step, s).start()
+
             for s in range(1, n_sec):
                 row_copy(s - 1, step, (s, gx, gz)).start()
         for step in range(STEPS):
             for s in range(1, n_sec):
                 row_copy(s - 1, step, (s, gx, gz)).wait_send()
+                pl.when(crossing)(row_over(step, s).wait_send)
 
     @pl.when(jnp.logical_not(is_source))
     def _():
@@ -283,21 +352,20 @@
         def from_sibling(step):
             return hand_on(1, step, pl.ds(sibling, 1), whole, near)
 
-        def to_partner(step):
-            return hand_on(2, step, pl.ds(gz, 1), pl.ds(part, 1), over)
-
         def from_partner(step):
-            return hand_on(2, step, pl.ds(partner, 1), pl.ds(part, 1), over)
+            return hand_on(2, step, pl.ds(partner, 1), crossed(step, part), over)
 
         def nearby_to_partner(step):
-            return hand_on(3, step, pl.ds(sibling, 1), pl.ds(part, 1), over)
+            return hand_on(3, step, pl.ds(sibling, 1), crossed(step, part), over)
 
         def nearby_from_partner(step):
-            return hand_on(3, step, pl.ds(3 - sibling, 1), pl.ds(part, 1), over)
+            return hand_on(3, step, pl.ds(3 - sibling, 1), crossed(step, part), over)
 
         def spread(step):
-            piece = held_rows.at[step, tiles(step), pl.ds(other, 2), pl.ds(part, 1)]
-            places = [near] + [(1 + o, gx, z) for o in others for z in (gz, sibling)]
+            piece = held_rows.at[step, tiles(step), pl.ds(other, 2), crossed(step, part)]
+            places = [near]
+            if step < STEPS - 1:
+                places += [(1 + o, gx, z) for o in others for z in (gz, sibling)]
             return [
                 pltpu.make_async_remote_copy(
                     piece, piece, row_send.at[i, step], row_recv.at[4 + part, step],
@@ -307,7 +375,8 @@
             ]
 
         def spread_in(step, which):
-            piece = held_rows.at[step, tiles(step), pl.ds(other, 2), pl.ds(which, 1)]
+            parts = pl.ds(which, 1) if step < STEPS - 1 else whole
+            piece = held_rows.at[step, tiles(step), pl.ds(other, 2), parts]
             return pltpu.make_async_remote_copy(
                 piece, piece, row_send.at[0, step], row_recv.at[4 + which, step],
                 device_id=near, device_id_type=MESH,
@@ -322,11 +391,11 @@
                 1: [v - DT * b * g for v, b, g in zip(get(1, start), buoyancy, slope_z)],
             }
 
-        def pressures(start):
+        def pressures(count, start):
             kappa, strength = get(6, start), get(7, start)
             spread = add(along_lanes(*get(0, start), lane), along_rows(grid, 1, start))
-            p, one, two = get(2, start), get(3, start), get(4, start)
-            for t in range(2):
+            p, one, two = (get(f, start)[:count] for f in (2, 3, 4))
+            for t in range(count):
                 load = kappa[t] * spread[t]
                 driven = strength[t] * load
                 one[t] = 0.9 * one[t] + (1.0 - 0.9) * 0.15 * driven
@@ -337,7 +406,8 @@
         def evolve(step):
             reach = 8 * (STEPS - step)
             chunks(OWN - reach, HIGH + reach, velocities, save)
-            chunks(OWN - reach + 8, HIGH + reach - 8, pressures, save)
+            count = 2 if step < STEPS - 1 else 1
+            chunks(OWN - reach + 8, HIGH + reach - 8, functools.partial(pressures, count), save)
 
         evolve(0)
 
@@ -349,7 +419,6 @@
 
         for step in range(STEPS):
             row_copy(0, step, near).wait_recv()
-            pl.when(crossing)(to_partner(step).start)
             to_sibling(step).start()
 
         def pass_on(step):
@@ -365,7 +434,7 @@
             if step < STEPS - 1:
                 pass_on(step + 1)
             pl.when(jnp.logical_not(crossing))(from_sibling(step).wait_recv)
-            for which in others:
+            for which in others if step < STEPS - 1 else []:
                 spread_in(step, which).wait_recv()
             pl.when(jnp.logical_not(crossing))(spread_in(step, part).wait_recv)
             low = OWN - 8 * (STEPS - 1 - step)
@@ -388,7 +457,6 @@
 
             @pl.when(crossing)
             def _():
-                to_partner(step).wait_send()
                 nearby_to_partner(step).wait_send()
                 for c in spread(step):
                     c.wait_send()
@@ -398,11 +466,6 @@
 
     pl.when(has_left)(each(left_copies, "wait_send"))
     pl.when(has_right)(each(right_copies, "wait_send"))
-
-    @pl.when(crossing)
-    def _():
-        pl.when(has_left)(corner_left.wait_send)
-        pl.when(has_right)(corner_right.wait_send)
 
 
 def solution(mesh):
@@ -424,8 +487,8 @@
                 pltpu.VMEM((STEPS, 2, 3, NPD, CELLS), jnp.float32),
                 pltpu.VMEM((STEPS, 2, 4, 3, NPD, CELLS), jnp.float32),
                 pltpu.VMEM((SPAN, CELLS), jnp.bfloat16),
-                pltpu.SemaphoreType.DMA((8,)),
-                pltpu.SemaphoreType.DMA((8,)),
+                pltpu.SemaphoreType.DMA((29,)),
+                pltpu.SemaphoreType.DMA((29,)),
                 pltpu.SemaphoreType.DMA((8, STEPS)),
                 pltpu.SemaphoreType.DMA((8, STEPS)),
             ],

time: 84.5 us -> 83 us (0.982)
  the two profiles are of different devices: /device:TPU:98 before, /device:TPU:34 now
where the time goes in v3:
time: 83 us; the launch traced here: 82.8 us
  Pallas kernels  81 us (98%)
  local copies, waits for them, and re-layouts  1.72 us (2%)
    pallas_call x1, Pallas kernels, local(): pl.pallas_call(functools.partial(solve, sizes), out_shape=jax.ShapeDtypeS...  81 us
    unnamed x1, local copies, waits for them, and re-layouts  1.72 us

profile of v3, /device:TPU:34, one launch (start us, length us, event | category | flops | bytes accessed | tf_op | source)
XLA Modules:
  0.0 82.8 jit_solution(17707462885865512864)
XLA Ops:
  0.0 81.0 %shard_map.46 = f32[5,128,128]{2,1,0:T(8,128)} custom-call(s32[32]{0:T(128)} %rows_ref.1, s32[3]{0:T(128)} %offset_ref.1, f32[5,128,128]{2,1,0:T(8,128)} %bitcast.4, f32[3,128,128]{2,1,0:T(8,128)} %bitcast.5), custom_call_target="tpu_custom_call" | custom-call | tf_op jit(solution)/shard_map/pallas_call | solution.py:477
  81.0 1.7 %copy.6 = f32[1,5,128,128]{3,2,1,0:T(8,128)} copy(f32[1,5,128,128]{3,2,1,0:T(8,128)} %bitcast.3) | data formatting | bytes 655360

commit v4 on v3

--- a/solution.py
+++ b/solution.py
@@ -54,17 +54,19 @@
 def chunks(low, high, body, save):
     count = (high - low) // CHUNK
 
-    def step(i, carry):
-        starts = [pl.multiple_of(low + (2 * i + j) * CHUNK, 8) for j in range(2)]
+    def run(first, size):
+        starts = [pl.multiple_of(low + (first + j) * CHUNK, 8) for j in range(size)]
         results = [body(start) for start in starts]
         for start, result in zip(starts, results):
             save(start, result)
+
+    def step(i, carry):
+        run(3 * i, 3)
         return carry
 
-    lax.fori_loop(0, count // 2, step, 0)
-    if count % 2:
-        start = low + (count - 1) * CHUNK
-        save(start, body(start))
+    lax.fori_loop(0, count // 3, step, 0)
+    if count % 3:
+        run(count - count % 3, count % 3)
 
 
 def solve(

time: 83 us -> 81.8 us (0.986)
  Pallas kernels: 81 us -> 79.8 us
    pallas_call x1, Pallas kernels: 81 us -> 79.8 us  [local(): pl.pallas_call(functools.partial(solve, sizes), out_shape=jax.ShapeDtypeS...]
where the time goes in v4:
time: 81.8 us; the launch traced here: 81.6 us
  Pallas kernels  79.8 us (98%)
  local copies, waits for them, and re-layouts  1.72 us (2%)
    pallas_call x1, Pallas kernels, local(): pl.pallas_call(functools.partial(solve, sizes), out_shape=jax.ShapeDtypeS...  79.8 us
    unnamed x1, local copies, waits for them, and re-layouts  1.72 us

profile of v4, /device:TPU:34, one launch (start us, length us, event | category | flops | bytes accessed | tf_op | source)
XLA Modules:
  0.0 81.6 jit_solution(15053510067065302500)
XLA Ops:
  0.0 79.8 %shard_map.46 = f32[5,128,128]{2,1,0:T(8,128)} custom-call(s32[32]{0:T(128)} %rows_ref.1, s32[3]{0:T(128)} %offset_ref.1, f32[5,128,128]{2,1,0:T(8,128)} %bitcast.4, f32[3,128,128]{2,1,0:T(8,128)} %bitcast.5), custom_call_target="tpu_custom_call" | custom-call | tf_op jit(solution)/shard_map/pallas_call | solution.py:479
  79.8 1.7 %copy.6 = f32[1,5,128,128]{3,2,1,0:T(8,128)} copy(f32[1,5,128,128]{3,2,1,0:T(8,128)} %bitcast.3) | data formatting | bytes 655360
